TPU v7x, 512 devices: a whole 4x4x16 slice. The times are simulated.
512 devices in a mesh: guide: 2 (over core), dp: 16 (over y, x), mp: 16 (over z).
Axes of the slice: x: 4, y: 4, z: 16, core: 2. Of those that a mesh axis runs over, the one named last changes fastest.
Arguments:
- states: bfloat16 [2, 128, 2048], P('guide', 'dp'), may hold values from -6 to 6
- lengths: int32 [2, 128], P('guide', 'dp'), may hold values from 1 to 32768, as said below
- sink_cache: bfloat16 [2, 128, 16, 2, 4, 128], P('guide', 'dp', 'mp'), may hold values from -48 to 48
- window_cache: bfloat16 [2, 128, 16, 2, 256, 128], P('guide', 'dp', 'mp'), may hold values from -360 to 360
- qkv_weight: bfloat16 [2048, 3, 16, 128], P(None, None, 'mp'), may hold values from -0.125 to 0.125
- out_weight: bfloat16 [16, 128, 2048], P('mp'), may hold values from -0.125 to 0.125
- expert_ids: int32 [2, 128, 8], replicated, may hold values from 0 to 63, all different within a row; in each aligned block of 8 rows (0 to 7, 8 to 15, ..., all dimensions but the last counted through in order) at most 2 rows name the same one
- route_weight: float32 [2, 128, 8], replicated, may hold values from 0.5 to 2
- expert_in: bfloat16 [2, 2048, 65536], P(None, None, ('guide', 'dp', 'mp')), may hold values from -0.125 to 0.125
- expert_out: bfloat16 [65536, 2048], P(('guide', 'dp', 'mp')), may hold values from -0.1875 to 0.1875
- vocab_weight: bfloat16 [2048, 26624], P(('guide', 'dp'), 'mp'), may hold values from -0.125 to 0.125
- guidance: float32 [128], P('dp'), may hold values from 1 to 5
Outputs:
- guided: float32 [128, 16, 2, 832], P('dp', 'mp', 'guide')
Inputs may be any that keep to these rules, and one draw needn't show every extreme that they name: `lengths`: one stream of one request has exactly 32768 cached positions. `expert_ids`: taking the tokens streams first, then requests, in aligned blocks of 8 tokens (the tokens of one device), no expert is named by more than 2 tokens of a block, a bound that some block reaches.
All inputs are finite; a program needn't handle non-finite values.
Results may differ from a plain program's by a relative error of at most 0.025.
Values may be sent and summed in bfloat16 or wider, within the bound.
A program may use at most 64 MiB of HBM per device.

v0:
```python
import math
import jax
import jax.numpy as jnp
from jax import lax
from jax.sharding import PartitionSpec as P

FFE = 1024
EPSILON = 1e-05


def partner(block, axis, stride):
    count = lax.axis_size(axis)
    route = []
    for low in range(count):
        high = low | 1 << stride
        if high != low and high < count:
            route += [(low, high), (high, low)]
    return lax.ppermute(block, axis, route)


def rms_norm(values):
    return values * lax.rsqrt(jnp.mean(values * values, axis=-1, keepdims=True) + EPSILON)


def rotate(vectors, positions):
    full_width = vectors.shape[-1]
    half_width = full_width // 2
    step_index = jnp.arange(half_width, dtype=jnp.float32)
    inverse = jnp.exp(step_index * (-2.0 * math.log(10000.0) / full_width))
    angles = positions.astype(jnp.float32)[:, None] * inverse[None, :]
    cosine = jnp.cos(angles)[:, None, :]
    sine_part = jnp.sin(angles)[:, None, :]
    first_half = vectors[..., :half_width]
    second = vectors[..., half_width:]
    return jnp.concatenate(
        [first_half * cosine - second * sine_part, second * cosine + first_half * sine_part],
        axis=-1,
    )


def body(
    states,
    lengths,
    sink_cache,
    window_cache,
    qkv_weight,
    out_weight,
    expert_ids,
    route_weight,
    expert_in,
    expert_out,
    vocab_weight,
    guidance,
):
    hidden = states[0]
    own_lengths = lengths[0]
    request_count = hidden.shape[0]
    normed = rms_norm(hidden.astype(jnp.float32)).astype(jnp.bfloat16)
    projected = jnp.einsum("rd,dthe->rthe", normed, qkv_weight, preferred_element_type=jnp.float32)
    query_rot = rotate(projected[:, 0], own_lengths).astype(jnp.bfloat16)
    fresh_key = rotate(projected[:, 1], own_lengths).astype(jnp.bfloat16)
    fresh_value = projected[:, 2].astype(jnp.bfloat16)
    sink_rows = sink_cache[0]
    window_rows = window_cache[0]
    sink_count = sink_rows.shape[3]
    window_count = window_rows.shape[3]
    root_size = math.sqrt(query_rot.shape[-1])
    sink_scores = (
        jnp.einsum(
            "rhe,rhse->rhs", query_rot, sink_rows[:, :, 0], preferred_element_type=jnp.float32
        )
        / root_size
    )
    window_scores = (
        jnp.einsum(
            "rhe,rhwe->rhw", query_rot, window_rows[:, :, 0], preferred_element_type=jnp.float32
        )
        / root_size
    )
    self_scores = (
        jnp.einsum("rhe,rhe->rh", query_rot, fresh_key, preferred_element_type=jnp.float32)
        / root_size
    )
    length_limit = own_lengths[:, None, None]
    sink_valid = jnp.arange(sink_count, dtype=jnp.int32)[None, None, :] < length_limit
    window_valid = (
        jnp.arange(window_count, dtype=jnp.int32)[None, None, :]
        >= sink_count + window_count - length_limit
    )
    sink_scores = jnp.where(sink_valid, sink_scores, -1e30)
    window_scores = jnp.where(window_valid, window_scores, -1e30)
    highest = jnp.maximum(
        jnp.maximum(jnp.max(sink_scores, axis=-1), jnp.max(window_scores, axis=-1)), self_scores
    )
    sink_exp = jnp.exp(sink_scores - highest[..., None])
    window_exp = jnp.exp(window_scores - highest[..., None])
    self_exp = jnp.exp(self_scores - highest)
    totals = jnp.sum(sink_exp, axis=-1) + jnp.sum(window_exp, axis=-1) + self_exp
    sink_prob = (sink_exp / totals[..., None]).astype(jnp.bfloat16)
    window_prob = (window_exp / totals[..., None]).astype(jnp.bfloat16)
    self_prob = (self_exp / totals).astype(jnp.bfloat16)
    mixture = (
        jnp.einsum(
            "rhs,rhse->rhe", sink_prob, sink_rows[:, :, 1], preferred_element_type=jnp.float32
        )
        + jnp.einsum(
            "rhw,rhwe->rhe", window_prob, window_rows[:, :, 1], preferred_element_type=jnp.float32
        )
        + self_prob[..., None].astype(jnp.float32) * fresh_value.astype(jnp.float32)
    ).astype(jnp.bfloat16)
    partial_out = jnp.einsum("rhe,hed->rd", mixture, out_weight, preferred_element_type=jnp.float32)
    attention_out = lax.psum(partial_out, "mp")
    residual = (hidden.astype(jnp.float32) + attention_out).astype(jnp.bfloat16)
    moe_in = rms_norm(residual.astype(jnp.float32)).astype(jnp.bfloat16)
    unit_count = expert_in.shape[2]
    unit_start = lax.axis_index(("guide", "dp", "mp")) * unit_count
    unit_expert = (unit_start + jnp.arange(unit_count, dtype=jnp.int32)) // FFE
    choice_rows = expert_ids.reshape(-1, expert_ids.shape[-1])
    route_rows = route_weight.reshape(-1, route_weight.shape[-1])
    coefficient = jnp.sum(
        jnp.where(
            choice_rows[:, :, None] == unit_expert[None, None, :], route_rows[:, :, None], 0.0
        ),
        axis=1,
    )
    piece = lax.all_gather(moe_in, ("guide", "dp"), axis=0, tiled=True)
    gate = jnp.dot(piece, expert_in[0], preferred_element_type=jnp.float32)
    upward = jnp.dot(piece, expert_in[1], preferred_element_type=jnp.float32)
    activated = (jax.nn.silu(gate) * upward * coefficient).astype(jnp.bfloat16)
    expert_terms = jnp.dot(activated, expert_out, preferred_element_type=jnp.float32)
    expert_part = lax.psum_scatter(expert_terms, ("guide", "dp"), scatter_dimension=0, tiled=True)
    expert_total = lax.psum(expert_part, "mp")
    final = rms_norm(residual.astype(jnp.float32) + expert_total).astype(jnp.bfloat16)
    final_all = lax.all_gather(final, ("guide", "dp"), axis=0, tiled=True)
    row_share = vocab_weight.shape[0]
    share_start = lax.axis_index(("guide", "dp")) * row_share
    final_cols = lax.dynamic_slice_in_dim(final_all, share_start, row_share, 1)
    logits = lax.psum_scatter(
        jnp.dot(final_cols, vocab_weight, preferred_element_type=jnp.float32).astype(jnp.bfloat16),
        ("guide", "dp"),
        scatter_dimension=0,
        tiled=True,
    ).astype(jnp.float32)
    half_width = logits.shape[1] // 2
    stream_index = lax.axis_index("guide")
    own_half = lax.dynamic_slice_in_dim(logits, stream_index * half_width, half_width, 1)
    other_half = lax.dynamic_slice_in_dim(logits, (1 - stream_index) * half_width, half_width, 1)
    partner_logits = partner(other_half, "guide", 0)
    is_conditional = stream_index == 0
    conditional = jnp.where(is_conditional, own_half, partner_logits)
    unconditional = jnp.where(is_conditional, partner_logits, own_half)
    guided = unconditional + guidance[:, None] * (conditional - unconditional)
    return guided.reshape(request_count, 1, 1, half_width)


def solution(mesh):
    in_specs = (
        P("guide", "dp", None),
        P("guide", "dp"),
        P("guide", "dp", "mp", None, None, None),
        P("guide", "dp", "mp", None, None, None),
        P(None, None, "mp", None),
        P("mp", None, None),
        P(),
        P(),
        P(None, None, ("guide", "dp", "mp")),
        P(("guide", "dp", "mp"), None),
        P(("guide", "dp"), "mp"),
        P("dp"),
    )
    out_specs = P("dp", "mp", "guide", None)
    return jax.shard_map(body, mesh=mesh, in_specs=in_specs, out_specs=out_specs, check_vma=False)
```

profile of v0, /device:TPU:1, one launch (start us, length us, event | category | flops | bytes accessed | tf_op | source)
XLA Modules:
  0.0 657.1 jit_solution(2036525778644055514)
XLA Ops:
  6.6 0.8 bitcast_convert_fusion
  7.4 0.8 broadcast_subtract_fusion
  8.2 0.9 fusion.23
  9.1 1.2 fusion
  10.5 0.2 fusion.6
  10.7 0.1 fusion.35
  10.9 0.2 fusion.57
  11.1 0.2 fusion.46
  11.4 0.2 fusion.37
  11.7 0.2 fusion.5
  12.0 0.1 fusion.36
  12.1 0.9 fusion.11
  13.0 128.0 %all-reduce.5.cloned.1.call-done = f32[8,2048]{1,0:T(8,128)} async-done(((f32[8,2048]{1,0:T(8,128)}), f32[8,2048]{1,0:T(8,128)}) %all-reduce.5.cloned.1.call-update) | async-done | bytes 65552 | tf_op jit(solution)/shard_map/psum | solution.py:112
  141.0 1.0 fusion.26
  142.0 0.7 fusion.27
  142.8 0.1 copy.24
  143.1 1.3 select_reduce_fusion
  144.4 65.6 %all-gather.3.cloned.1.call-done = bf16[256,2048]{1,0:T(8,128)(2,1)} async-done(((bf16[8,2048]{1,0:T(8,128)(2,1)}), bf16[256,2048]{1,0:T(8,128)(2,1)}) %all-gather.3.cloned.1.call-update) | async-done | bytes 1048592 | tf_op jit(solution)/shard_map/all_gather | solution.py:126
  210.0 1.9 fusion.9
  211.9 3.2 fusion.4
  215.2 99.4 %reduce-scatter.2.cloned.1.call-done = f32[8,2048]{1,0:T(8,128)} async-done(((f32[256,2048]{1,0:T(8,128)}), f32[8,2048]{1,0:T(8,128)}) %reduce-scatter.2.cloned.1.call-update) | async-done | bytes 65552 | tf_op jit(solution)/shard_map/reduce_scatter | solution.py:131
  314.6 125.9 %all-reduce.7.cloned.1.call-done = f32[8,2048]{1,0:T(8,128)} async-done(((f32[8,2048]{1,0:T(8,128)}), f32[8,2048]{1,0:T(8,128)}) %all-reduce.7.cloned.1.call-update) | async-done | bytes 65552 | tf_op jit(solution)/shard_map/psum | solution.py:132
  440.5 1.0 multiply_reduce_fusion
  441.5 1.5 multiply_convert_fusion
  443.1 65.8 %all-gather.5.cloned.1.call-done = bf16[256,2048]{1,0:T(8,128)(2,1)} async-done(((bf16[8,2048]{1,0:T(8,128)(2,1)}), bf16[256,2048]{1,0:T(8,128)(2,1)}) %all-gather.5.cloned.1.call-update) | async-done | bytes 1048592 | tf_op jit(solution)/shard_map/all_gather | solution.py:134
  508.9 2.2 convolution_convert_fusion
  511.1 1.3 dynamic-slice
  513.1 132.5 %all-reduce.9.cloned.1.call-done = bf16[256,1664]{1,0:T(8,128)(2,1)} async-done(((bf16[256,1664]{1,0:T(8,128)(2,1)}), bf16[256,1664]{1,0:T(8,128)(2,1)}) %all-reduce.9.cloned.1.call-update) | async-done | bytes 851984
  645.6 0.7 dynamic-slice_convert_fusion
  646.4 2.3 collective-permute-start
  648.7 0.8 collective-permute-done
  649.6 0.6 copy.26
  (56 shorter events, 1.3 us)
Async XLA Ops:
  6.5 2.5 copy-start
  6.5 4.8 copy-start.9
  6.5 3.9 copy-start.5
  6.5 4.2 copy-start.11
  6.5 5.6 copy-start.3
  6.5 134.5 %all-reduce.5.cloned.1.call-start = ((), (), s32[]{:S(2)}) async-start(), calls=%async_computation.1 | async-start | bytes 131072 | tf_op jit(solution)/shard_map/psum | solution.py:112
  9.1 131.9 %copy-start.4 = (bf16[1,8,2048]{2,1,0:T(8,128)(2,1)S(1)}, bf16[1,8,2048]{2,1,0:T(8,128)(2,1)}, u32[]{:S(2)}) copy-start(bf16[1,8,2048]{2,1,0:T(8,128)(2,1)} %param.12) | copy-start | bytes 98308
  9.1 133.7 %copy-start.7 = (s32[2,128,8]{1,2,0:T(8,128)S(1)}, s32[2,128,8]{1,2,0:T(8,128)}, u32[]{:S(2)}) copy-start(s32[2,128,8]{1,2,0:T(8,128)} %param.18) | copy-start | bytes 24580
  10.3 132.6 %copy-start.8 = (f32[2,128,8]{1,2,0:T(8,128)S(1)}, f32[2,128,8]{1,2,0:T(8,128)}, u32[]{:S(2)}) copy-start(f32[2,128,8]{1,2,0:T(8,128)} %param.19) | copy-start | bytes 24580
  12.1 199.8 %copy-start.2 = (bf16[128,2048]{1,0:T(8,128)(2,1)S(1)}, bf16[128,2048]{1,0:T(8,128)(2,1)}, u32[]{:S(2)}) copy-start(bf16[128,2048]{1,0:T(8,128)(2,1)} %param.21) | copy-start | bytes 1572868
  13.0 197.0 %all-gather.3.cloned.1.call-start = ((), (), s32[]{:S(2)}) async-start(), calls=%async_computation.2 | async-start | bytes 1081344 | tf_op jit(solution)/shard_map/all_gather | solution.py:126
  142.7 171.9 %reduce-scatter.2.cloned.1.call-start = ((), (), s32[]{:S(2)}) async-start(), calls=%async_computation.3 | async-start | bytes 2162688 | tf_op jit(solution)/shard_map/reduce_scatter | solution.py:131
  210.0 1.9 copy-start.1
  215.1 293.8 %copy-start.6 = (bf16[64,1664]{1,0:T(8,128)(2,1)S(1)}, bf16[64,1664]{1,0:T(8,128)(2,1)}, u32[]{:S(2)}) copy-start(bf16[64,1664]{1,0:T(8,128)(2,1)} %param.22) | copy-start | bytes 638980
  215.1 434.4 %copy-start.10 = (f32[8]{0:T(128)S(1)}, f32[8]{0:T(128)}, u32[]{:S(2)}) copy-start(f32[8]{0:T(128)} %param.23) | copy-start | bytes 100
  215.1 225.4 %all-reduce.7.cloned.1.call-start = ((), (), s32[]{:S(2)}) async-start(), calls=%async_computation.4 | async-start | bytes 131072 | tf_op jit(solution)/shard_map/psum | solution.py:132
  314.6 194.3 %all-gather.5.cloned.1.call-start = ((), (), s32[]{:S(2)}) async-start(), calls=%async_computation.5 | async-start | bytes 1081344 | tf_op jit(solution)/shard_map/all_gather | solution.py:134
  443.1 202.6 %all-reduce.9.cloned.1.call-start = ((), (), s32[]{:S(2)}) async-start(), calls=%async_computation.6 | async-start | bytes 1703936
  646.4 3.1 collective-permute-start
Sparse Core Ops, SparseCore 0:
  13.1 127.8 all-reduce.4
  144.7 65.3 all-gather.2
  215.3 99.2 reduce-scatter.1
  316.9 123.6 all-reduce.6
  443.6 65.3 all-gather.4
  512.1 133.5 all-reduce.8
where the time goes:
time: 658 us; the launch traced here: 657 us
  waiting for transfers between devices  618 us (94%)
  between operations  14.4 us (2%)
  matrix products  9.92 us (2%)
  other arithmetic  9.7 us (1%)
    unnamed x7, waiting for transfers between devices  133 us
    psum x1, waiting for transfers between devices, body(): attention_out = lax.psum(partial_out, 'mp')  128 us
    psum x1, waiting for transfers between devices, body(): expert_total = lax.psum(expert_part, 'mp')  126 us
    reduce_scatter x1, waiting for transfers between devices, body(): lax.psum_scatter(expert_terms, ('guide', 'dp'), scatter_dimension=0, tile...  99.4 us
    all_gather x1, waiting for transfers between devices, body(): final_all = lax.all_gather(final, ('guide', 'dp'), axis=0, tiled=True)  65.8 us
    all_gather x1, waiting for transfers between devices, body(): piece = lax.all_gather(moe_in, ('guide', 'dp'), axis=0, tiled=True)  65.6 us
  transfers between devices with their start and end apart: 7, of which 7 were waited for; matrix products, arithmetic and copies ran while one was open for 0% of the time, Pallas kernels for 0%

commit v1 on v0

--- a/solution.py
+++ b/solution.py
@@ -129,7 +129,11 @@
     activated = (jax.nn.silu(gate) * upward * coefficient).astype(jnp.bfloat16)
     expert_terms = jnp.dot(activated, expert_out, preferred_element_type=jnp.float32)
     expert_part = lax.psum_scatter(expert_terms, ("guide", "dp"), scatter_dimension=0, tiled=True)
-    expert_total = lax.psum(expert_part, "mp")
+    expert_total = expert_part
+    for hop in (1, 2, 4, 8):
+        expert_total = expert_total + lax.ppermute(
+            expert_total, "mp", [(dev, dev ^ hop) for dev in range(16)]
+        )
     final = rms_norm(residual.astype(jnp.float32) + expert_total).astype(jnp.bfloat16)
     final_all = lax.all_gather(final, ("guide", "dp"), axis=0, tiled=True)
     row_share = vocab_weight.shape[0]

time: 658 us -> 566 us (0.86)
  waiting for transfers between devices: 618 us -> 498 us
  starting transfers between devices: 2.5 us -> 31.8 us
    psum x1 -> x0, waiting for transfers between devices: 126 us -> none  [body(): expert_total = lax.psum(expert_part, 'mp')]
    ppermute x0 -> x4, starting transfers between devices: none -> 29.4 us  [body(): lax.ppermute(expert_total, 'mp', [(dev, dev ^ hop) for dev in range(16)])]
    ppermute x0 -> x4, waiting for transfers between devices: none -> 7.08 us  [body(): lax.ppermute(expert_total, 'mp', [(dev, dev ^ hop) for dev in range(16)])]
    unnamed x7 -> x6, waiting for transfers between devices: 133 us -> 133 us
  transfers between devices with their start and end apart: 7 -> 10, of which waited for: 7 -> 10; matrix products, arithmetic and copies ran while one was open for 0% -> 1% of each run, Pallas kernels for 0% -> 0%
where the time goes in v1:
time: 566 us; the launch traced here: 565 us
  waiting for transfers between devices  498 us (88%)
  starting transfers between devices  31.8 us (6%)
  between operations  14.1 us (2%)
  matrix products  9.92 us (2%)
  other arithmetic  8.89 us (2%)
    unnamed x6, waiting for transfers between devices  133 us
    psum x1, waiting for transfers between devices, body(): attention_out = lax.psum(partial_out, 'mp')  128 us
    reduce_scatter x1, waiting for transfers between devices, body(): lax.psum_scatter(expert_terms, ('guide', 'dp'), scatter_dimension=0, tile...  99.4 us
    all_gather x1, waiting for transfers between devices, body(): piece = lax.all_gather(moe_in, ('guide', 'dp'), axis=0, tiled=True)  65.6 us
    all_gather x1, waiting for transfers between devices, body(): final_all = lax.all_gather(final, ('guide', 'dp'), axis=0, tiled=True)  64 us
    ppermute x4, starting transfers between devices, body(): lax.ppermute(expert_total, 'mp', [(dev, dev ^ hop) for dev in range(16)])  29.4 us
  transfers between devices with their start and end apart: 10, of which 10 were waited for; matrix products, arithmetic and copies ran while one was open for 1% of the time, Pallas kernels for 0%

profile of v1, /device:TPU:1, one launch (start us, length us, event | category | flops | bytes accessed | tf_op | source)
XLA Modules:
  0.0 565.1 jit_solution(5490239403724983815)
XLA Ops:
  6.6 0.8 bitcast_convert_fusion
  7.4 0.8 broadcast_subtract_fusion
  8.2 0.9 fusion.23
  9.1 1.2 fusion
  10.5 0.2 fusion.6
  12.1 0.9 fusion.11
  13.0 128.0 %all-reduce.4.cloned.1.call-done = f32[8,2048]{1,0:T(8,128)} async-done(((f32[8,2048]{1,0:T(8,128)}), f32[8,2048]{1,0:T(8,128)}) %all-reduce.4.cloned.1.call-update) | async-done | bytes 65552 | tf_op jit(solution)/shard_map/psum | solution.py:112
  141.0 1.0 fusion.26
  142.0 0.7 fusion.27
  143.1 1.3 select_reduce_fusion
  144.4 65.6 %all-gather.3.cloned.1.call-done = bf16[256,2048]{1,0:T(8,128)(2,1)} async-done(((bf16[8,2048]{1,0:T(8,128)(2,1)}), bf16[256,2048]{1,0:T(8,128)(2,1)}) %all-gather.3.cloned.1.call-update) | async-done | bytes 1048592 | tf_op jit(solution)/shard_map/all_gather | solution.py:126
  210.0 1.9 fusion.9
  211.9 3.2 fusion.4
  215.2 99.4 %reduce-scatter.2.cloned.1.call-done = f32[8,2048]{1,0:T(8,128)} async-done(((f32[256,2048]{1,0:T(8,128)}), f32[8,2048]{1,0:T(8,128)}) %reduce-scatter.2.cloned.1.call-update) | async-done | bytes 65552 | tf_op jit(solution)/shard_map/reduce_scatter | solution.py:131
  314.6 3.1 collective-permute-start
  317.7 2.1 collective-permute-done
  319.8 0.8 add.124
  320.6 4.2 collective-permute-start.1
  324.8 1.7 collective-permute-done.1
  326.5 7.4 %collective-permute-start.2 = (f32[8,2048]{1,0:T(8,128)S(1)}, f32[8,2048]{1,0:T(8,128)S(1)}, u32[]{:S(2)}, u32[]{:S(2)}) collective-permute-start(f32[8,2048]{1,0:T(8,128)S(1)} %add.125), channel_id=1, source_target_pairs={{0,4},{1,5},{2,6},{3,7},{4,0},{5,1},{6,2},{7,3},{8,12},{9,13},{10,... | collective-permute-start | bytes 196616 | tf_op jit(solution)/shard_map/ppermute | solution.py:134
  333.9 1.6 collective-permute-done.2
  335.6 14.7 %collective-permute-start.3 = (f32[8,2048]{1,0:T(8,128)S(1)}, f32[8,2048]{1,0:T(8,128)S(1)}, u32[]{:S(2)}, u32[]{:S(2)}) collective-permute-start(f32[8,2048]{1,0:T(8,128)S(1)} %add.126), channel_id=1, source_target_pairs={{0,8},{1,9},{2,10},{3,11},{4,12},{5,13},{6,14},{7,15},{8,0},{9,1},... | collective-permute-start | bytes 196616 | tf_op jit(solution)/shard_map/ppermute | solution.py:134
  350.3 1.6 collective-permute-done.3
  352.1 0.7 multiply_convert_fusion
  352.8 64.0 %all-gather.5.cloned.1.call-done = bf16[256,2048]{1,0:T(8,128)(2,1)} async-done(((bf16[8,2048]{1,0:T(8,128)(2,1)}), bf16[256,2048]{1,0:T(8,128)(2,1)}) %all-gather.5.cloned.1.call-update) | async-done | bytes 1048592 | tf_op jit(solution)/shard_map/all_gather | solution.py:138
  416.9 2.2 convolution_convert_fusion
  419.1 1.3 dynamic-slice
  421.0 132.9 %all-reduce.6.cloned.1.call-done = bf16[256,1664]{1,0:T(8,128)(2,1)} async-done(((bf16[256,1664]{1,0:T(8,128)(2,1)}), bf16[256,1664]{1,0:T(8,128)(2,1)}) %all-reduce.6.cloned.1.call-update) | async-done | bytes 851984
  553.9 0.7 dynamic-slice_convert_fusion
  554.7 2.3 collective-permute-start.4
  557.0 0.8 collective-permute-done.4
  557.9 0.6 copy.26
  (64 shorter events, 2.5 us)
Async XLA Ops:
  6.5 2.5 copy-start
  6.5 4.8 copy-start.9
  6.5 3.9 copy-start.5
  6.5 4.2 copy-start.11
  6.5 5.6 copy-start.3
  6.5 134.5 %all-reduce.4.cloned.1.call-start = ((), (), s32[]{:S(2)}) async-start(), calls=%async_computation.1 | async-start | bytes 131072 | tf_op jit(solution)/shard_map/psum | solution.py:112
  9.1 131.9 %copy-start.4 = (bf16[1,8,2048]{2,1,0:T(8,128)(2,1)S(1)}, bf16[1,8,2048]{2,1,0:T(8,128)(2,1)}, u32[]{:S(2)}) copy-start(bf16[1,8,2048]{2,1,0:T(8,128)(2,1)} %param.12) | copy-start | bytes 98308
  9.1 133.7 %copy-start.7 = (s32[2,128,8]{1,2,0:T(8,128)S(1)}, s32[2,128,8]{1,2,0:T(8,128)}, u32[]{:S(2)}) copy-start(s32[2,128,8]{1,2,0:T(8,128)} %param.18) | copy-start | bytes 24580
  10.3 132.6 %copy-start.8 = (f32[2,128,8]{1,2,0:T(8,128)S(1)}, f32[2,128,8]{1,2,0:T(8,128)}, u32[]{:S(2)}) copy-start(f32[2,128,8]{1,2,0:T(8,128)} %param.19) | copy-start | bytes 24580
  12.1 199.8 %copy-start.2 = (bf16[128,2048]{1,0:T(8,128)(2,1)S(1)}, bf16[128,2048]{1,0:T(8,128)(2,1)}, u32[]{:S(2)}) copy-start(bf16[128,2048]{1,0:T(8,128)(2,1)} %param.21) | copy-start | bytes 1572868
  13.0 197.0 %all-gather.3.cloned.1.call-start = ((), (), s32[]{:S(2)}) async-start(), calls=%async_computation.2 | async-start | bytes 1081344 | tf_op jit(solution)/shard_map/all_gather | solution.py:126
  142.7 171.9 %reduce-scatter.2.cloned.1.call-start = ((), (), s32[]{:S(2)}) async-start(), calls=%async_computation.3 | async-start | bytes 2162688 | tf_op jit(solution)/shard_map/reduce_scatter | solution.py:131
  210.0 1.9 copy-start.1
  215.1 201.8 %copy-start.6 = (bf16[64,1664]{1,0:T(8,128)(2,1)S(1)}, bf16[64,1664]{1,0:T(8,128)(2,1)}, u32[]{:S(2)}) copy-start(bf16[64,1664]{1,0:T(8,128)(2,1)} %param.22) | copy-start | bytes 638980
  215.1 342.7 %copy-start.10 = (f32[8]{0:T(128)S(1)}, f32[8]{0:T(128)}, u32[]{:S(2)}) copy-start(f32[8]{0:T(128)} %param.23) | copy-start | bytes 100
  215.1 201.7 %all-gather.5.cloned.1.call-start = ((), (), s32[]{:S(2)}) async-start(), calls=%async_computation.4 | async-start | bytes 1081344 | tf_op jit(solution)/shard_map/all_gather | solution.py:138
  314.6 5.2 collective-permute-start
  320.6 5.9 %collective-permute-start.1 = (f32[8,2048]{1,0:T(8,128)S(1)}, f32[8,2048]{1,0:T(8,128)S(1)}, u32[]{:S(2)}, u32[]{:S(2)}) collective-permute-start(f32[8,2048]{1,0:T(8,128)S(1)} %add.124), channel_id=1, source_target_pairs={{0,2},{1,3},{2,0},{3,1},{4,6},{5,7},{6,4},{7,5},{8,10},{9,11},{10,... | collective-permute-start | bytes 196616 | tf_op jit(solution)/shard_map/ppermute | solution.py:134
  326.5 9.0 %collective-permute-start.2 = (f32[8,2048]{1,0:T(8,128)S(1)}, f32[8,2048]{1,0:T(8,128)S(1)}, u32[]{:S(2)}, u32[]{:S(2)}) collective-permute-start(f32[8,2048]{1,0:T(8,128)S(1)} %add.125), channel_id=1, source_target_pairs={{0,4},{1,5},{2,6},{3,7},{4,0},{5,1},{6,2},{7,3},{8,12},{9,13},{10,... | collective-permute-start | bytes 196616 | tf_op jit(solution)/shard_map/ppermute | solution.py:134
  335.6 16.4 %collective-permute-start.3 = (f32[8,2048]{1,0:T(8,128)S(1)}, f32[8,2048]{1,0:T(8,128)S(1)}, u32[]{:S(2)}, u32[]{:S(2)}) collective-permute-start(f32[8,2048]{1,0:T(8,128)S(1)} %add.126), channel_id=1, source_target_pairs={{0,8},{1,9},{2,10},{3,11},{4,12},{5,13},{6,14},{7,15},{8,0},{9,1},... | collective-permute-start | bytes 196616 | tf_op jit(solution)/shard_map/ppermute | solution.py:134
  352.8 201.1 %all-reduce.6.cloned.1.call-start = ((), (), s32[]{:S(2)}) async-start(), calls=%async_computation.5 | async-start | bytes 1703936
  554.7 3.1 collective-permute-start.4
Sparse Core Ops, SparseCore 0:
  13.1 127.8 all-reduce.3
  144.7 65.3 all-gather.2
  215.3 99.2 reduce-scatter.1
  352.9 63.9 all-gather.4
  420.4 133.5 all-reduce.5
